TPU v7x, 512 devices: a whole 4x8x8 slice. The times are simulated.
512 devices in a mesh: grp: 16 (over y, core), ops: 32 (over x, z).
Axes of the slice: x: 4, y: 8, z: 8, core: 2. Of those that a mesh axis runs over, the one named last changes fastest.
Arguments:
- op_embed: bfloat16 [131072, 256], P(('grp', 'ops')), may hold values from -6 to 6
- machine_embed: bfloat16 [8192, 256], P('grp'), may hold values from -6 to 6
- cotangent: bfloat16 [131072, 256], P(('grp', 'ops')), may hold values from -6 to 6
- w_query: bfloat16 [256, 256], replicated, may hold values from -0.375 to 0.375
- w_key: bfloat16 [256, 256], replicated, may hold values from -0.375 to 0.375
- w_value: bfloat16 [256, 256], replicated, may hold values from -0.375 to 0.375
- slot_local: int32 [512, 16], P(('grp', 'ops')), may hold values from 0 to 3
- counts: int32 [131072, 16], P(('grp', 'ops')), may hold values from 0 to 128, as said below
Outputs:
- op_grad: bfloat16 [131072, 256], P(('grp', 'ops'))
- machine_grad: float32 [8192, 256], P(('grp', 'ops'))
- grad_wq: float32 [256, 256], replicated
- grad_wk: float32 [256, 256], replicated
- grad_wv: float32 [256, 256], replicated
Inputs may be any that keep to these rules, and one draw needn't show every extreme that they name: The eligible machines of slot e's block for operation o are its first counts[o, e] machines; 0 means the operation has no eligible machine in that block.
All inputs are finite; a program needn't handle non-finite values.
Results may differ from a plain program's by a relative error of at most 0.0056.
Values may be sent and summed in bfloat16 or wider, within the bound.
No kernel may reach another device: no remote copies, remote signals or barrier semaphores. Data moves between devices by JAX's collectives and lax.ppermute only.
A program may use at most 64 MiB of HBM per device.

v0:
```python
import jax
import jax.numpy as jnp
from jax import lax
from jax.sharding import PartitionSpec as P

HEADS = 8
BLK = 128
mean_scale = 0.08838834764831845


def slot_grads(queries, cotangent4, key_rows, value_rows, lengths):
    head_size = queries.shape[2]
    inv_root = head_size ** (-0.5)
    scores = (
        jnp.einsum("ohc,mhc->ohm", queries, key_rows, preferred_element_type=jnp.float32) * inv_root
    )
    sigmoid_score = jax.nn.sigmoid(scores)
    columns = lax.broadcasted_iota(jnp.int32, scores.shape, 2)
    eligible = columns < lengths[:, None, None]
    gates = jnp.where(eligible, sigmoid_score, 0.0).astype(jnp.bfloat16)
    value_dot = jnp.einsum(
        "ohc,mhc->ohm", cotangent4, value_rows, preferred_element_type=jnp.float32
    )
    dscore = jnp.where(
        eligible, mean_scale * value_dot * sigmoid_score * (1.0 - sigmoid_score) * inv_root, 0.0
    ).astype(jnp.bfloat16)
    query_part = jnp.einsum("ohm,mhc->ohc", dscore, key_rows, preferred_element_type=jnp.float32)
    key_grad = jnp.einsum(
        "ohm,ohc->mhc", dscore, queries, preferred_element_type=jnp.float32
    ).astype(jnp.bfloat16)
    value_grad = (
        mean_scale
        * jnp.einsum("ohm,ohc->mhc", gates, cotangent4, preferred_element_type=jnp.float32)
    ).astype(jnp.bfloat16)
    return (query_part, key_grad, value_grad)


def per_device(op_embed, machine_embed, cotangent, w_query, w_key, w_value, slot_local, counts):
    groups = lax.axis_size("grp")
    ops_count = op_embed.shape[0]
    model_width = op_embed.shape[1]
    head_size = model_width // HEADS
    machine_rows = machine_embed.shape[0]
    blocks_here = machine_rows // BLK
    highest = lax.Precision.HIGHEST
    both_weights = jnp.concatenate([w_key, w_value], axis=1)
    queries = jnp.dot(op_embed, w_query, preferred_element_type=jnp.float32).astype(jnp.bfloat16)
    wanted = lax.all_to_all(
        slot_local.reshape(groups, 1), "grp", split_axis=0, concat_axis=0, tiled=True
    )
    wanted_ids = wanted[:, 0]
    picker = wanted_ids[:, None] == jnp.arange(blocks_here, dtype=jnp.int32)[None, :]
    local_pairs = jnp.dot(machine_embed, both_weights, preferred_element_type=jnp.float32).astype(
        jnp.bfloat16
    )
    outgoing = local_pairs.reshape(blocks_here, BLK, 2 * model_width)[wanted_ids]
    fetched = lax.all_to_all(outgoing, "grp", split_axis=0, concat_axis=0, tiled=True)
    key_slots = fetched[:, :, :model_width].reshape(groups, BLK, HEADS, head_size)
    value_slots = fetched[:, :, model_width:].reshape(groups, BLK, HEADS, head_size)
    query_heads = queries.reshape(ops_count, HEADS, head_size)
    cot_heads = cotangent.reshape(ops_count, HEADS, head_size)

    def per_slot(summed_q, pieces):
        key_rows, value_rows, lengths = pieces
        query_part, key_grad, value_grad = slot_grads(
            query_heads, cot_heads, key_rows, value_rows, lengths
        )
        return (
            summed_q + query_part,
            (key_grad.reshape(BLK, model_width), value_grad.reshape(BLK, model_width)),
        )

    start_q = jnp.zeros((ops_count, HEADS, head_size), jnp.float32)
    summed_q, (key_grads, value_grads) = lax.scan(
        per_slot, start_q, (key_slots, value_slots, counts.T)
    )
    grad_query = summed_q.astype(jnp.bfloat16).reshape(ops_count, model_width)
    op_grad = (
        cotangent.astype(jnp.float32)
        + jnp.dot(grad_query, w_query.T, preferred_element_type=jnp.float32)
    ).astype(jnp.bfloat16)
    wq_term = jnp.einsum("od,oe->de", op_embed, grad_query, preferred_element_type=jnp.float32)
    returned = lax.all_to_all(
        jnp.concatenate([key_grads, value_grads], axis=2),
        "grp",
        split_axis=0,
        concat_axis=0,
        tiled=True,
    )
    summed = jnp.einsum(
        "gb,gr->br",
        picker.astype(jnp.bfloat16),
        returned.reshape(groups, BLK * 2 * model_width),
        preferred_element_type=jnp.float32,
    )
    summed = summed.reshape(machine_rows, 2 * model_width)
    key_total = summed[:, :model_width]
    value_total = summed[:, model_width:]
    machine_part = jnp.dot(key_total, w_key.astype(jnp.float32).T, precision=highest) + jnp.dot(
        value_total, w_value.astype(jnp.float32).T, precision=highest
    )
    embed_f = machine_embed.astype(jnp.float32)
    wk_term = jnp.dot(embed_f.T, key_total, precision=highest)
    wv_term = jnp.dot(embed_f.T, value_total, precision=highest)
    summed_total = lax.psum(machine_part, "ops")
    share_rows = machine_rows // lax.axis_size("ops")
    first_row = lax.axis_index("ops") * share_rows
    machine_grad = lax.dynamic_slice_in_dim(summed_total, first_row, share_rows, 0)
    weight_sums = lax.psum((wq_term, wk_term, wv_term), ("grp", "ops"))
    shard_count = float(groups * lax.axis_size("ops"))
    grad_wq = weight_sums[0] / shard_count
    grad_wk = weight_sums[1] / shard_count
    grad_wv = weight_sums[2] / shard_count
    return (op_grad, machine_grad, grad_wq, grad_wk, grad_wv)


def solution(mesh):
    return jax.shard_map(
        per_device,
        mesh=mesh,
        in_specs=(
            P(("grp", "ops"), None),
            P("grp", None),
            P(("grp", "ops"), None),
            P(),
            P(),
            P(),
            P(("grp", "ops"), None),
            P(("grp", "ops"), None),
        ),
        out_specs=(P(("grp", "ops"), None), P(("grp", "ops"), None), P(), P(), P()),
        check_vma=False,
    )
```

profile of v0, /device:TPU:8, one launch (start us, length us, event | category | flops | bytes accessed | tf_op | source)
XLA Modules:
  0.0 657.2 jit_solution(9235457132968034616)
XLA Ops:
  7.2 1.4 copy.46
  8.6 9.1 %all-to-all-start = ((s32[16,1,1]{2,1,0:T(1,128)}), s32[16,1,1]{2,1,0:T(1,128)S(1)}, u32[]{:S(2)}, u32[]{:S(2)}) async-start(s32[16,1,1]{2,1,0:T(1,128)} %copy.46), calls=%async_computation | async-start | bytes 16384 | tf_op jit(solution)/shard_map/all_to_all | solution.py:48
  18.9 4.9 all-to-all-done
  24.2 2.0 gather_fusion
  26.2 5.1 all-to-all-start.1
  31.7 46.8 %all-to-all-done.1 = bf16[16,128,512]{2,1,0:T(8,128)(2,1)S(1)} async-done(((bf16[16,128,512]{2,1,0:T(8,128)(2,1)}), bf16[16,128,512]{2,1,0:T(8,128)(2,1)S(1)}, u32[]{:S(2)}, u32[]{:S(2)}) %all-to-all-start.1) | async-done | bytes 2097184 | tf_op jit(solution)/shard_map/all_to_all | solution.py:57
  78.6 1.6 fusion.38
  80.2 1.7 copy.47
  81.9 1.3 copy.48
  83.2 63.6 %while.15 = (s32[]{:T(128)}, f32[256,8,32]{0,2,1:T(8,128)S(1)}, bf16[16,128,256]{1,2,0:T(8,128)(2,1)}, bf16[16,128,256]{1,2,0:T(8,128)(2,1)}, bf16[16,128,8,32]{...) while((s32[]{:T(128)}, f32[256,8,32]{0,2,1:T(8,128)S(1)}, ...), condition=%wide.region_1.2_spmd.clone, body=%wide.region_0.1_spmd.clone.sunk | while | flops 87785472 | bytes 6361235 | solution.py:74
  84.4 1.3 fusion.80
  88.4 1.3 fusion.80
  92.4 1.3 fusion.80
  96.3 1.3 fusion.80
  100.3 1.3 fusion.80
  104.3 1.3 fusion.80
  108.2 1.3 fusion.80
  112.2 1.3 fusion.80
  116.2 1.3 fusion.80
  120.2 1.3 fusion.80
  124.1 1.3 fusion.80
  128.1 1.3 fusion.80
  132.1 1.3 fusion.80
  140.1 1.3 fusion.80
  144.0 1.3 fusion.80
  146.8 3.1 pad_maximum_fusion
  149.9 6.9 %all-to-all-start.2 = ((bf16[16,128,512]{1,2,0:T(8,128)(2,1)}), bf16[16,128,512]{1,2,0:T(8,128)(2,1)}, u32[]{:S(2)}, u32[]{:S(2)}) async-start(bf16[16,128,512]{1,2,0:T(8,128)(2,1)} %pad_maximum_fusion), calls=%async_computation.2 | async-start | bytes 4194304 | tf_op jit(solution)/shard_map/all_to_all | solution.py:83
  157.7 46.3 %all-to-all-done.2 = bf16[16,128,512]{1,2,0:T(8,128)(2,1)} async-done(((bf16[16,128,512]{1,2,0:T(8,128)(2,1)}), bf16[16,128,512]{1,2,0:T(8,128)(2,1)}, u32[]{:S(2)}, u32[]{:S(2)}) %all-to-all-start.2) | async-done | bytes 2097184 | tf_op jit(solution)/shard_map/all_to_all | solution.py:83
  204.0 3.4 copy.57
  214.0 274.6 %all-reduce.6.cloned.1.call-done = (f32[256,256]{0,1:T(8,128)}, f32[256,256]{0,1:T(8,128)}, f32[256,256]{0,1:T(8,128)}) async-done(((f32[256,256]{0,1:T(8,128)}, f32[256,256]{0,1:T(8,128)}, f32[256,256]{0,1:T(8,128)}), (f32[256,256]{0,1:T(8,128)}, f32[256,256]{0,1:T(8,128)}, f32[256,256]{0,1:T(8,128)})) %all-reduce.6.cloned.1.call-update) | async-done | bytes 786448 | tf_op jit(solution)/shard_map/psum | solution.py:109
  493.2 155.8 %all-reduce.4.cloned.1.call-done = f32[512,256]{1,0:T(8,128)} async-done(((f32[512,256]{1,0:T(8,128)}), f32[512,256]{1,0:T(8,128)}) %all-reduce.4.cloned.1.call-update) | async-done | bytes 524304 | tf_op jit(solution)/shard_map/psum | solution.py:105
  649.0 1.3 constant_dynamic-slice_fusion.1
  (144 shorter events, 57.5 us)
Async XLA Ops:
  7.2 10.5 %copy-start = (bf16[512,256]{1,0:T(8,128)(2,1)S(1)}, bf16[512,256]{1,0:T(8,128)(2,1)}, u32[]{:S(2)}) copy-start(bf16[512,256]{1,0:T(8,128)(2,1)} %param.11) | copy-start | bytes 786436
  8.6 15.3 %all-to-all-start = ((s32[16,1,1]{2,1,0:T(1,128)}), s32[16,1,1]{2,1,0:T(1,128)S(1)}, u32[]{:S(2)}, u32[]{:S(2)}) async-start(s32[16,1,1]{2,1,0:T(1,128)} %copy.46), calls=%async_computation | async-start | bytes 16384 | tf_op jit(solution)/shard_map/all_to_all | solution.py:48
  26.2 5.1 copy-start.6
  26.2 5.3 copy-start.2
  26.2 5.3 copy-start.4
  26.2 52.3 %all-to-all-start.1 = ((bf16[16,128,512]{2,1,0:T(8,128)(2,1)}), bf16[16,128,512]{2,1,0:T(8,128)(2,1)S(1)}, u32[]{:S(2)}, u32[]{:S(2)}) async-start(bf16[16,128,512]{2,1,0:T(8,128)(2,1)} %gather_fusion), calls=%async_computation.1 | async-start | bytes 4194304 | tf_op jit(solution)/shard_map/all_to_all | solution.py:57
  80.2 1.7 copy-start.1
  149.9 6.9 %copy-start.3 = (bf16[256,256]{1,0:T(8,128)(2,1)S(1)}, bf16[256,256]{1,0:T(8,128)(2,1)}, u32[]{:S(2)}) copy-start(bf16[256,256]{1,0:T(8,128)(2,1)} %param.10) | copy-start | bytes 393220
  149.9 54.2 %all-to-all-start.2 = ((bf16[16,128,512]{1,2,0:T(8,128)(2,1)}), bf16[16,128,512]{1,2,0:T(8,128)(2,1)}, u32[]{:S(2)}, u32[]{:S(2)}) async-start(bf16[16,128,512]{1,2,0:T(8,128)(2,1)} %pad_maximum_fusion), calls=%async_computation.2 | async-start | bytes 4194304 | tf_op jit(solution)/shard_map/all_to_all | solution.py:83
  156.8 331.9 %all-reduce.6.cloned.1.call-start = ((), (), s32[]{:S(2)}) async-start(), calls=%async_computation.4 | async-start | bytes 1572864 | tf_op jit(solution)/shard_map/psum | solution.py:109
  208.0 3.4 copy-start.8
  208.7 3.1 copy-start.9
  211.3 1.8 copy-start.5
  211.3 1.8 copy-start.7
  211.4 437.6 %all-reduce.4.cloned.1.call-start = ((), (), s32[]{:S(2)}) async-start(), calls=%async_computation.3 | async-start | bytes 1048576 | tf_op jit(solution)/shard_map/psum | solution.py:105
Sparse Core Ops, SparseCore 0:
  211.5 277.0 all-reduce.5
  492.0 156.9 all-reduce.3
where the time goes:
time: 659 us; the launch traced here: 657 us
  waiting for transfers between devices  529 us (80%)
  matrix products  48.8 us (7%)
  local copies, waits for them, and re-layouts  38.4 us (6%)
  starting transfers between devices  21.1 us (3%)
  between operations  14.3 us (2%)
    psum x1, waiting for transfers between devices, per_device(): weight_sums = lax.psum((wq_term, wk_term, wv_term), ('grp', 'ops'))  275 us
    psum x1, waiting for transfers between devices, per_device(): summed_total = lax.psum(machine_part, 'ops')  156 us
    all_to_all x1, waiting for transfers between devices, per_device(): lax.all_to_all(outgoing, 'grp', split_axis=0, concat_axis=0, tiled=True)  46.8 us
    all_to_all x1, waiting for transfers between devices, per_device(): lax.all_to_all(jnp.concatenate([key_grads, value_grads], axis=2), 'grp',...  46.3 us
    dot_general x16, matrix products, slot_grads(): jnp.einsum('ohc,mhc->ohm', cotangent4, value_rows, preferred_element_type...  20.9 us
  transfers between devices with their start and end apart: 5, of which 5 were waited for; matrix products, arithmetic and copies ran while one was open for 1% of the time, Pallas kernels for 0%

commit v1 on v0

--- a/solution.py
+++ b/solution.py
@@ -102,7 +102,11 @@
     embed_f = machine_embed.astype(jnp.float32)
     wk_term = jnp.dot(embed_f.T, key_total, precision=highest)
     wv_term = jnp.dot(embed_f.T, value_total, precision=highest)
-    summed_total = lax.psum(machine_part, "ops")
+    summed_total = machine_part
+    for hop in (1, 2, 4, 8, 16):
+        summed_total = summed_total + lax.ppermute(
+            summed_total, "ops", [(dev, dev ^ hop) for dev in range(32)]
+        )
     share_rows = machine_rows // lax.axis_size("ops")
     first_row = lax.axis_index("ops") * share_rows
     machine_grad = lax.dynamic_slice_in_dim(summed_total, first_row, share_rows, 0)

time: 659 us -> 596 us (0.904)
  the two profiles are of different devices: /device:TPU:8 before, /device:TPU:17 now
where the time goes in v1:
time: 596 us; the launch traced here: 593 us
  waiting for transfers between devices  379 us (64%)
  matrix products  62.6 us (11%)
  blocking collectives  54.9 us (9%)
  starting transfers between devices  40 us (7%)
  local copies, waits for them, and re-layouts  37.4 us (6%)
  between operations  14.3 us (2%)
    psum x1, waiting for transfers between devices, per_device(): weight_sums = lax.psum((wq_term, wk_term, wv_term), ('grp', 'ops'))  264 us
    ppermute x5, waiting for transfers between devices, per_device(): lax.ppermute(summed_total, 'ops', [(dev, dev ^ hop) for dev in range(32)])  64.1 us
    all_to_all x1, blocking collectives, per_device(): lax.all_to_all(jnp.concatenate([key_grads, value_grads], axis=2), 'grp',...  54.9 us
    all_to_all x1, waiting for transfers between devices, per_device(): lax.all_to_all(outgoing, 'grp', split_axis=0, concat_axis=0, tiled=True)  47.1 us
    ppermute x5, starting transfers between devices, per_device(): lax.ppermute(summed_total, 'ops', [(dev, dev ^ hop) for dev in range(32)])  23.7 us
    dot_general x16, matrix products, slot_grads(): jnp.einsum('ohc,mhc->ohm', queries, key_rows, preferred_element_type=jnp....  21.3 us
    dot_general x16, matrix products, slot_grads(): jnp.einsum('ohm,mhc->ohc', dscore, key_rows, preferred_element_type=jnp.f...  17 us
  transfers between devices with their start and end apart: 8, of which 7 were waited for; matrix products, arithmetic and copies ran while one was open for 2% of the time, Pallas kernels for 0%

profile of v1, /device:TPU:17, one launch (start us, length us, event | category | flops | bytes accessed | tf_op | source)
XLA Modules:
  0.0 593.3 jit_solution(13893918019098432157)
XLA Ops:
  7.2 1.4 copy.46
  8.6 9.2 %all-to-all-start = ((s32[16,1,1]{2,1,0:T(1,128)}), s32[16,1,1]{2,1,0:T(1,128)S(1)}, u32[]{:S(2)}, u32[]{:S(2)}) async-start(s32[16,1,1]{2,1,0:T(1,128)} %copy.46), calls=%async_computation | async-start | bytes 16384 | tf_op jit(solution)/shard_map/all_to_all | solution.py:48
  19.1 3.8 all-to-all-done
  23.2 2.0 gather_fusion
  25.2 6.9 %all-to-all-start.1 = ((bf16[16,128,512]{2,1,0:T(8,128)(2,1)}), bf16[16,128,512]{2,1,0:T(8,128)(2,1)}, u32[]{:S(2)}, u32[]{:S(2)}) async-start(bf16[16,128,512]{2,1,0:T(8,128)(2,1)} %gather_fusion), calls=%async_computation.1 | async-start | bytes 4194304 | tf_op jit(solution)/shard_map/all_to_all | solution.py:57
  32.6 47.1 %all-to-all-done.1 = bf16[16,128,512]{2,1,0:T(8,128)(2,1)} async-done(((bf16[16,128,512]{2,1,0:T(8,128)(2,1)}), bf16[16,128,512]{2,1,0:T(8,128)(2,1)}, u32[]{:S(2)}, u32[]{:S(2)}) %all-to-all-start.1) | async-done | bytes 2097184 | tf_op jit(solution)/shard_map/all_to_all | solution.py:57
  79.8 1.7 fusion.38
  83.4 77.3 %while.15 = (s32[]{:T(128)}, f32[256,8,32]{0,2,1:T(8,128)S(1)}, bf16[16,128,256]{1,2,0:T(8,128)(2,1)}, bf16[16,128,256]{1,2,0:T(8,128)(2,1)}, bf16[16,128,8,32]{...) while((s32[]{:T(128)}, f32[256,8,32]{0,2,1:T(8,128)S(1)}, ...), condition=%wide.region_1.2_spmd.clone, body=%wide.region_0.1_spmd.clone.sunk | while | flops 87785472 | bytes 6361235 | solution.py:74
  83.4 1.3 fusion.79
  88.3 1.3 fusion.79
  93.1 1.3 fusion.79
  97.9 1.3 fusion.79
  102.8 1.3 fusion.79
  107.6 1.3 fusion.79
  112.4 1.3 fusion.79
  117.3 1.3 fusion.79
  131.8 1.3 fusion.79
  160.7 1.7 pad_maximum_fusion
  162.5 54.9 %all_to_all.22 = bf16[16,128,512]{1,2,0:T(8,128)(2,1)} all-to-all(bf16[16,128,512]{1,2,0:T(8,128)(2,1)S(1)} %pad_maximum_fusion), channel_id=1, replica_groups=mesh['grp'=16,'ops'=32] {'grp'}, dimensions={0} | all-to-all | bytes 4194304 | tf_op jit(solution)/shard_map/all_to_all | solution.py:83
  217.4 3.4 copy.57
  220.8 1.6 fusion.34
  222.4 2.0 reshape.79
  225.2 2.4 collective-permute-start
  227.7 12.5 %collective-permute-done = f32[512,256]{1,0:T(8,128)S(1)} collective-permute-done((f32[512,256]{1,0:T(8,128)S(1)}, f32[512,256]{1,0:T(8,128)S(1)}, u32[]{:S(2)}, u32[]{:S(2)}) %collective-permute-start) | collective-permute-done | bytes 524320 | tf_op jit(solution)/shard_map/ppermute | solution.py:107
  240.3 5.2 collective-permute-start.1
  245.4 22.7 %collective-permute-done.1 = f32[512,256]{1,0:T(8,128)S(1)} collective-permute-done((f32[512,256]{1,0:T(8,128)S(1)}, f32[512,256]{1,0:T(8,128)S(1)}, u32[]{:S(2)}, u32[]{:S(2)}) %collective-permute-start.1) | collective-permute-done | bytes 524320 | tf_op jit(solution)/shard_map/ppermute | solution.py:107
  268.2 8.1 %collective-permute-start.2 = (f32[512,256]{1,0:T(8,128)S(1)}, f32[512,256]{1,0:T(8,128)S(1)}, u32[]{:S(2)}, u32[]{:S(2)}) collective-permute-start(f32[512,256]{1,0:T(8,128)S(1)} %add.56), channel_id=1, source_target_pairs={{0,4},{1,5},{2,6},{3,7},{4,0},{5,1},{6,2},{7,3},{8,12},{9,13},{10,... | collective-permute-start | bytes 1572872 | tf_op jit(solution)/shard_map/ppermute | solution.py:107
  277.3 21.3 %collective-permute-done.2 = f32[512,256]{1,0:T(8,128)S(1)} collective-permute-done((f32[512,256]{1,0:T(8,128)S(1)}, f32[512,256]{1,0:T(8,128)S(1)}, u32[]{:S(2)}, u32[]{:S(2)}) %collective-permute-start.2) | collective-permute-done | bytes 524320 | tf_op jit(solution)/shard_map/ppermute | solution.py:107
  298.7 3.3 collective-permute-start.3
  304.6 7.5 %collective-permute-done.3 = f32[512,256]{1,0:T(8,128)S(1)} collective-permute-done((f32[512,256]{1,0:T(8,128)S(1)}, f32[512,256]{1,0:T(8,128)S(1)}, u32[]{:S(2)}, u32[]{:S(2)}) %collective-permute-start.3) | collective-permute-done | bytes 524320 | tf_op jit(solution)/shard_map/ppermute | solution.py:107
  312.2 4.7 collective-permute-start.4
  317.8 263.5 %all-reduce.3.cloned.1.call-done = (f32[256,256]{0,1:T(8,128)}, f32[256,256]{0,1:T(8,128)}, f32[256,256]{0,1:T(8,128)}) async-done(((f32[256,256]{0,1:T(8,128)}, f32[256,256]{0,1:T(8,128)}, f32[256,256]{0,1:T(8,128)}), (f32[256,256]{0,1:T(8,128)}, f32[256,256]{0,1:T(8,128)}, f32[256,256]{0,1:T(8,128)})) %all-reduce.3.cloned.1.call-update) | async-done | bytes 786448 | tf_op jit(solution)/shard_map/psum | solution.py:113
  (150 shorter events, 79.5 us)
Async XLA Ops:
  7.2 10.6 %copy-start = (bf16[512,256]{1,0:T(8,128)(2,1)S(1)}, bf16[512,256]{1,0:T(8,128)(2,1)}, u32[]{:S(2)}) copy-start(bf16[512,256]{1,0:T(8,128)(2,1)} %param.11) | copy-start | bytes 786436
  8.6 14.3 %all-to-all-start = ((s32[16,1,1]{2,1,0:T(1,128)}), s32[16,1,1]{2,1,0:T(1,128)S(1)}, u32[]{:S(2)}, u32[]{:S(2)}) async-start(s32[16,1,1]{2,1,0:T(1,128)} %copy.46), calls=%async_computation | async-start | bytes 16384 | tf_op jit(solution)/shard_map/all_to_all | solution.py:48
  25.2 7.0 %copy-start.4 = (bf16[256,256]{1,0:T(8,128)(2,1)S(1)}, bf16[256,256]{1,0:T(8,128)(2,1)}, u32[]{:S(2)}) copy-start(bf16[256,256]{1,0:T(8,128)(2,1)} %param.12) | copy-start | bytes 393220
  25.2 7.1 %copy-start.1 = (bf16[256,256]{1,0:T(8,128)(2,1)S(1)}, bf16[256,256]{1,0:T(8,128)(2,1)}, u32[]{:S(2)}) copy-start(bf16[256,256]{1,0:T(8,128)(2,1)} %param.10) | copy-start | bytes 393220
  25.2 7.1 %copy-start.2 = (bf16[256,256]{1,0:T(8,128)(2,1)S(1)}, bf16[256,256]{1,0:T(8,128)(2,1)}, u32[]{:S(2)}) copy-start(bf16[256,256]{1,0:T(8,128)(2,1)} %param.13) | copy-start | bytes 393220
  25.2 54.5 %all-to-all-start.1 = ((bf16[16,128,512]{2,1,0:T(8,128)(2,1)}), bf16[16,128,512]{2,1,0:T(8,128)(2,1)}, u32[]{:S(2)}, u32[]{:S(2)}) async-start(bf16[16,128,512]{2,1,0:T(8,128)(2,1)} %gather_fusion), calls=%async_computation.1 | async-start | bytes 4194304 | tf_op jit(solution)/shard_map/all_to_all | solution.py:57
  32.2 549.1 %all-reduce.3.cloned.1.call-start = ((), (), s32[]{:S(2)}) async-start(), calls=%async_computation.3 | async-start | bytes 1572864 | tf_op jit(solution)/shard_map/psum | solution.py:113
  220.8 3.6 copy-start.6
  222.3 2.4 copy-start.7
  225.2 15.0 %collective-permute-start = (f32[512,256]{1,0:T(8,128)S(1)}, f32[512,256]{1,0:T(8,128)S(1)}, u32[]{:S(2)}, u32[]{:S(2)}) collective-permute-start(f32[512,256]{1,0:T(8,128)S(1)} %convolution_add_fusion), channel_id=1, source_target_pairs={{0,1},{1,0},{2,3},{3,2},{4,5},{5,4},{6,7},{7,6},{8,9},{9,8},{10,11... | collective-permute-start | bytes 1572872 | tf_op jit(solution)/shard_map/ppermute | solution.py:107
  240.3 27.9 %collective-permute-start.1 = (f32[512,256]{1,0:T(8,128)S(1)}, f32[512,256]{1,0:T(8,128)S(1)}, u32[]{:S(2)}, u32[]{:S(2)}) collective-permute-start(f32[512,256]{1,0:T(8,128)S(1)} %add.55), channel_id=1, source_target_pairs={{0,2},{1,3},{2,0},{3,1},{4,6},{5,7},{6,4},{7,5},{8,10},{9,11},{10,... | collective-permute-start | bytes 1572872 | tf_op jit(solution)/shard_map/ppermute | solution.py:107
  268.2 30.4 %collective-permute-start.2 = (f32[512,256]{1,0:T(8,128)S(1)}, f32[512,256]{1,0:T(8,128)S(1)}, u32[]{:S(2)}, u32[]{:S(2)}) collective-permute-start(f32[512,256]{1,0:T(8,128)S(1)} %add.56), channel_id=1, source_target_pairs={{0,4},{1,5},{2,6},{3,7},{4,0},{5,1},{6,2},{7,3},{8,12},{9,13},{10,... | collective-permute-start | bytes 1572872 | tf_op jit(solution)/shard_map/ppermute | solution.py:107
  298.7 18.2 %copy-start.3 = (bf16[256,256]{1,0:T(8,128)(2,1)S(1)}, bf16[256,256]{1,0:T(8,128)(2,1)}, u32[]{:S(2)}) copy-start(bf16[256,256]{1,0:T(8,128)(2,1)} %param.13) | copy-start | bytes 393220
  298.7 18.2 %copy-start.5 = (bf16[256,256]{1,0:T(8,128)(2,1)S(1)}, bf16[256,256]{1,0:T(8,128)(2,1)}, u32[]{:S(2)}) copy-start(bf16[256,256]{1,0:T(8,128)(2,1)} %param.12) | copy-start | bytes 393220
  298.7 13.5 %collective-permute-start.3 = (f32[512,256]{1,0:T(8,128)S(1)}, f32[512,256]{1,0:T(8,128)S(1)}, u32[]{:S(2)}, u32[]{:S(2)}) collective-permute-start(f32[512,256]{1,0:T(8,128)S(1)} %add.57), channel_id=1, source_target_pairs={{0,8},{1,9},{2,10},{3,11},{4,12},{5,13},{6,14},{7,15},{8,0},{9,1},... | collective-permute-start | bytes 1572872 | tf_op jit(solution)/shard_map/ppermute | solution.py:107
  312.2 273.7 %collective-permute-start.4 = (f32[512,256]{1,0:T(8,128)S(1)}, f32[512,256]{1,0:T(8,128)S(1)}, u32[]{:S(2)}, u32[]{:S(2)}) collective-permute-start(f32[512,256]{1,0:T(8,128)S(1)} %add.58), channel_id=1, source_target_pairs={{0,16},{1,17},{2,18},{3,19},{4,20},{5,21},{6,22},{7,23},{8,24},{9,... | collective-permute-start | bytes 1572872 | tf_op jit(solution)/shard_map/ppermute | solution.py:107
Sparse Core Ops, SparseCore 0:
  304.7 276.5 all-reduce.2
